TPU v7x, 512 devices: a whole 4x4x16 slice. The times are simulated.
512 devices in a mesh: pipe: 8 (over x, core), dp: 64 (over y, z).
Axes of the slice: x: 4, y: 4, z: 16, core: 2. Of those that a mesh axis runs over, the one named last changes fastest.
Arguments:
- saved_inputs: bfloat16 [8, 8192, 8192], P('pipe', 'dp'), may hold values from -1000 to 1000
- cotangent: bfloat16 [8192, 8192], P('dp', 'pipe'), may hold values from -500 to 500
- weights_bf16: bfloat16 [8, 2, 64, 8192], P('pipe', None, None, 'dp'), may hold values from -6 to 6
- master: float32 [8, 2, 64, 8192], P('pipe', None, None, 'dp'), may hold values from -6 to 6
- moment1: float32 [8, 2, 64, 8192], P('pipe', None, None, 'dp'), may hold values from -6 to 6
- moment2: float32 [8, 2, 64, 8192], P('pipe', None, None, 'dp'), may hold values from 0.5 to 8
- valid_rows: int32 [64], P('dp'), may hold values from 1 to 128, 6144 in all
Outputs:
- new_master: float32 [8, 2, 64, 8192], P('pipe', None, None, 'dp')
- new_moment1: float32 [8, 2, 64, 8192], P('pipe', None, None, 'dp')
- new_moment2: float32 [8, 2, 64, 8192], P('pipe', None, None, 'dp')
- new_weights: bfloat16 [8, 2, 64, 8192], P('pipe', None, None, 'dp')
Inputs may be any that keep to these rules, and one draw needn't show every extreme that they name: `valid_rows`: the counts sum to 6144.
All inputs are finite; a program needn't handle non-finite values. No bound on the sum of `valid_rows` on one device may be relied on, other than what follows from the above.
Results may differ from a plain program's by a relative error of at most 0.02.
Values may be sent and summed in bfloat16 or wider, within the bound.
No kernel may reach another device: no remote copies, remote signals or barrier semaphores. Data moves between devices by JAX's collectives and lax.ppermute only.
A program may use at most 64 MiB of HBM per device.

v0:
```python
import math
import jax
import jax.numpy as jnp
from jax import lax
from jax.sharding import PartitionSpec as P

BETA_ONE = 0.9
BETA_TWO = 0.95
LEARN_RATE = 0.05
DECAY_RATE = 0.1
ADAM_EPS = 1e-08
CLIP_RMS = 2.0
NORM_EPS = 1e-12


def shifted(x, axis, by):
    length = lax.axis_size(axis)
    pairs = [(i, i + by) for i in range(length) if 0 <= i + by < length]
    return lax.ppermute(x, axis, pairs)


def section_backward(inputs_block, incoming, weights):
    down_proj = weights[0]
    up_proj = weights[1]
    model_width = inputs_block.shape[1]
    adapter_rank = weights.shape[1]
    pre_act = lax.dot_general(
        inputs_block, down_proj, (((1,), (1,)), ((), ())), preferred_element_type=jnp.float32
    ) * (1.0 / math.sqrt(model_width))
    activated = jax.nn.silu(pre_act).astype(jnp.bfloat16)
    logistic = jax.nn.sigmoid(pre_act)
    derivative = logistic * (1.0 + pre_act * (1.0 - logistic))
    along_rank = lax.dot_general(
        incoming, up_proj, (((1,), (1,)), ((), ())), preferred_element_type=jnp.float32
    ) * (1.0 / math.sqrt(adapter_rank))
    back_grad = (along_rank * derivative).astype(jnp.bfloat16)
    grad_up = lax.dot_general(
        activated, incoming, (((0,), (0,)), ((), ())), preferred_element_type=jnp.float32
    ) * (1.0 / math.sqrt(adapter_rank))
    grad_down = lax.dot_general(
        back_grad, inputs_block, (((0,), (0,)), ((), ())), preferred_element_type=jnp.float32
    ) * (1.0 / math.sqrt(model_width))
    outgoing = (
        incoming.astype(jnp.float32)
        + jnp.dot(back_grad, down_proj, preferred_element_type=jnp.float32)
        * (1.0 / math.sqrt(model_width))
    ).astype(jnp.bfloat16)
    return (outgoing, jnp.stack([grad_down, grad_up]))


def body(saved_inputs, cotangent, weights_bf16, master, moment1, moment2, valid_rows):
    sections = lax.axis_size("pipe")
    section_index = lax.axis_index("pipe")
    weights = lax.all_gather(weights_bf16[0], "dp", axis=2, tiled=True)
    loss_grad = lax.all_gather(cotangent, "pipe", axis=1, tiled=True)
    inputs = saved_inputs[0]
    row_count = inputs.shape[0]
    model_width = inputs.shape[1]
    adapter_rank = weights.shape[1]
    live_rows = jnp.arange(row_count, dtype=jnp.int32) < valid_rows[0]
    loss_grad = jnp.where(live_rows[:, None], loss_grad, jnp.zeros_like(loss_grad))
    blocks = 1
    block_rows = row_count // blocks
    grad_shape = (2, adapter_rank, model_width)

    def chain_turn(step_index, state_pair):
        gradients, received = state_pair
        position = step_index - (sections - 1 - section_index)
        active = (position >= 0) & (position < blocks)
        incoming = jnp.where(section_index == sections - 1, loss_grad, received)

        def compute():
            return section_backward(inputs, incoming, weights)

        def skipped():
            return (
                jnp.zeros((block_rows, model_width), jnp.bfloat16),
                jnp.zeros(grad_shape, jnp.float32),
            )

        outgoing, grad_part = lax.cond(active, compute, skipped)
        received = shifted(outgoing, "pipe", -1)
        return (gradients + grad_part, received)

    start_pair = (
        jnp.zeros(grad_shape, jnp.float32),
        jnp.zeros((block_rows, model_width), jnp.bfloat16),
    )
    gradients, unused = lax.fori_loop(0, sections + blocks - 1, chain_turn, start_pair)
    grad_shard = lax.psum_scatter(gradients, "dp", scatter_dimension=2, tiled=True)
    square_sum = lax.psum(jnp.sum(grad_shard * grad_shard), ("pipe", "dp"))
    norm_limit = CLIP_RMS * math.sqrt(2.0 * sections * adapter_rank * model_width)
    clip_factor = jnp.minimum(1.0, norm_limit / jnp.sqrt(square_sum + NORM_EPS))
    scaled = grad_shard * clip_factor
    new_moment1 = BETA_ONE * moment1[0] + (1.0 - BETA_ONE) * scaled
    new_moment2 = BETA_TWO * moment2[0] + (1.0 - BETA_TWO) * scaled * scaled
    new_master = master[0] - LEARN_RATE * (
        new_moment1 / (jnp.sqrt(new_moment2) + ADAM_EPS) + DECAY_RATE * master[0]
    )
    return (
        new_master[None],
        new_moment1[None],
        new_moment2[None],
        new_master.astype(jnp.bfloat16)[None],
    )


def solution(mesh):
    in_specs = (
        P("pipe", "dp", None),
        P("dp", "pipe"),
        P("pipe", None, None, "dp"),
        P("pipe", None, None, "dp"),
        P("pipe", None, None, "dp"),
        P("pipe", None, None, "dp"),
        P("dp"),
    )
    out_specs = (
        P("pipe", None, None, "dp"),
        P("pipe", None, None, "dp"),
        P("pipe", None, None, "dp"),
        P("pipe", None, None, "dp"),
    )
    return jax.shard_map(body, mesh=mesh, in_specs=in_specs, out_specs=out_specs, check_vma=False)
```

profile of v0, /device:TPU:1, one launch (start us, length us, event | category | flops | bytes accessed | tf_op | source)
XLA Modules:
  0.0 1259.6 jit_solution(12248657878223781486)
XLA Ops:
  9.4 39.3 %all-gather.4.cloned.1.call-done = bf16[128,8192]{1,0:T(8,128)(2,1)} async-done(((bf16[128,1024]{1,0:T(8,128)(2,1)}), bf16[128,8192]{1,0:T(8,128)(2,1)}) %all-gather.4.cloned.1.call-update) | async-done | bytes 2097168 | tf_op jit(solution)/shard_map/all_gather | solution.py:55
  48.7 3.1 broadcast_select_fusion.1
  51.8 126.0 %all-gather.6.cloned.1.call-done = bf16[1,2,64,8192]{3,2,1,0:T(8,128)(2,1)} async-done(((bf16[1,2,64,128]{3,2,1,0:T(8,128)(2,1)}), bf16[1,2,64,8192]{3,2,1,0:T(8,128)(2,1)}) %all-gather.6.cloned.1.call-update) | async-done | bytes 2097168 | tf_op jit(solution)/shard_map/all_gather | solution.py:54
  179.3 272.9 %while.18 = (s32[]{:T(128)}, f32[2,64,8192]{2,1,0:T(8,128)}, bf16[128,8192]{1,0:T(8,128)(2,1)}, s32[]{:T(128)}, pred[]{:T(512)}, /*index=5*/bf16[128,8192]{1,0:T...) while((s32[]{:T(128)}, f32[2,64,8192]{2,1,0:T(8,128)}, ...), condition=%wide.region_3.4_spmd.clone, body=%wide.region_0.3_spmd.clone.sunk | while | flops 680656896 | bytes 72499496 | solution.py:89
  179.3 3.9 conditional.3
  179.3 2.4 broadcast.35
  183.3 11.6 collective-permute-start
  194.9 4.7 select_add_fusion.2
  199.5 20.4 %collective-permute-done = bf16[128,8192]{1,0:T(8,128)(2,1)} collective-permute-done((bf16[128,8192]{1,0:T(8,128)(2,1)}, bf16[128,8192]{1,0:T(8,128)(2,1)}, u32[]{:S(2)}, u32[]{:S(2)}) %collective-permute-start) | collective-permute-done | bytes 2097184 | tf_op jit(solution)/shard_map/while/body/eval_jaxpr/ppermute | solution.py:19
  220.0 3.9 conditional.3
  220.0 2.4 broadcast.35
  223.9 1.9 collective-permute-start
  225.8 5.9 select_add_fusion.2
  231.7 19.8 %collective-permute-done = bf16[128,8192]{1,0:T(8,128)(2,1)} collective-permute-done((bf16[128,8192]{1,0:T(8,128)(2,1)}, bf16[128,8192]{1,0:T(8,128)(2,1)}, u32[]{:S(2)}, u32[]{:S(2)}) %collective-permute-start) | collective-permute-done | bytes 2097184 | tf_op jit(solution)/shard_map/while/body/eval_jaxpr/ppermute | solution.py:19
  251.5 3.9 conditional.3
  251.5 2.4 broadcast.35
  255.4 1.9 collective-permute-start
  257.3 5.9 select_add_fusion.2
  263.3 19.8 %collective-permute-done = bf16[128,8192]{1,0:T(8,128)(2,1)} collective-permute-done((bf16[128,8192]{1,0:T(8,128)(2,1)}, bf16[128,8192]{1,0:T(8,128)(2,1)}, u32[]{:S(2)}, u32[]{:S(2)}) %collective-permute-start) | collective-permute-done | bytes 2097184 | tf_op jit(solution)/shard_map/while/body/eval_jaxpr/ppermute | solution.py:19
  283.1 3.9 conditional.3
  283.1 2.4 broadcast.35
  287.0 1.9 collective-permute-start
  288.9 5.9 select_add_fusion.2
  294.9 19.8 %collective-permute-done = bf16[128,8192]{1,0:T(8,128)(2,1)} collective-permute-done((bf16[128,8192]{1,0:T(8,128)(2,1)}, bf16[128,8192]{1,0:T(8,128)(2,1)}, u32[]{:S(2)}, u32[]{:S(2)}) %collective-permute-start) | collective-permute-done | bytes 2097184 | tf_op jit(solution)/shard_map/while/body/eval_jaxpr/ppermute | solution.py:19
  314.7 3.9 conditional.3
  314.7 2.4 broadcast.35
  318.6 1.9 collective-permute-start
  320.5 5.9 select_add_fusion.2
  326.4 19.8 %collective-permute-done = bf16[128,8192]{1,0:T(8,128)(2,1)} collective-permute-done((bf16[128,8192]{1,0:T(8,128)(2,1)}, bf16[128,8192]{1,0:T(8,128)(2,1)}, u32[]{:S(2)}, u32[]{:S(2)}) %collective-permute-start) | collective-permute-done | bytes 2097184 | tf_op jit(solution)/shard_map/while/body/eval_jaxpr/ppermute | solution.py:19
  346.2 3.9 conditional.3
  346.2 2.4 broadcast.35
  350.1 1.9 collective-permute-start
  352.1 5.9 select_add_fusion.2
  358.0 24.5 %collective-permute-done = bf16[128,8192]{1,0:T(8,128)(2,1)} collective-permute-done((bf16[128,8192]{1,0:T(8,128)(2,1)}, bf16[128,8192]{1,0:T(8,128)(2,1)}, u32[]{:S(2)}, u32[]{:S(2)}) %collective-permute-start) | collective-permute-done | bytes 2097184 | tf_op jit(solution)/shard_map/while/body/eval_jaxpr/ppermute | solution.py:19
  382.5 10.5 conditional.3
  382.5 2.2 convolution_multiply_fusion.3
  384.8 2.0 broadcast_select_fusion
  388.8 2.3 pad_maximum_fusion
  391.0 2.0 fusion.1
  393.0 1.9 collective-permute-start
  395.0 5.9 select_add_fusion.2
  400.9 19.8 %collective-permute-done = bf16[128,8192]{1,0:T(8,128)(2,1)} collective-permute-done((bf16[128,8192]{1,0:T(8,128)(2,1)}, bf16[128,8192]{1,0:T(8,128)(2,1)}, u32[]{:S(2)}, u32[]{:S(2)}) %collective-permute-start) | collective-permute-done | bytes 2097184 | tf_op jit(solution)/shard_map/while/body/eval_jaxpr/ppermute | solution.py:19
  420.7 3.9 conditional.3
  420.7 2.4 broadcast.35
  426.5 5.9 select_add_fusion.2
  432.5 19.8 %collective-permute-done = bf16[128,8192]{1,0:T(8,128)(2,1)} collective-permute-done((bf16[128,8192]{1,0:T(8,128)(2,1)}, bf16[128,8192]{1,0:T(8,128)(2,1)}, u32[]{:S(2)}, u32[]{:S(2)}) %collective-permute-start) | collective-permute-done | bytes 2097184 | tf_op jit(solution)/shard_map/while/body/eval_jaxpr/ppermute | solution.py:19
  452.3 684.5 %reduce-scatter.2.cloned.1.call-done = f32[2,64,128]{2,1,0:T(8,128)} async-done(((f32[2,64,8192]{2,1,0:T(8,128)}), f32[2,64,128]{2,1,0:T(8,128)}) %reduce-scatter.2.cloned.1.call-update) | async-done | bytes 65552 | tf_op jit(solution)/shard_map/reduce_scatter | solution.py:90
  1138.2 112.5 %psum.7 = f32[]{:T(128)} all-reduce(f32[]{:T(128)} %multiply_reduce_fusion), channel_id=1, replica_groups=mesh['pipe'=8,'dp'=64] {'pipe','dp'}, use_global_device_ids=true, to_apply=%region_6.7 | all-reduce | flops 1 | bytes 8 | tf_op jit(solution)/shard_map/psum | solution.py:91
  (34 shorter events, 20.5 us)
Async XLA Ops:
  7.2 41.5 %all-gather.4.cloned.1.call-start = ((), (), s32[]{:S(2)}) async-start(), calls=%async_computation.1 | async-start | bytes 2359296 | tf_op jit(solution)/shard_map/all_gather | solution.py:55
  7.9 169.9 %all-gather.6.cloned.1.call-start = ((), (), s32[]{:S(2)}) async-start(), calls=%async_computation.3 | async-start | bytes 2129920 | tf_op jit(solution)/shard_map/all_gather | solution.py:54
  8.6 1128.1 %reduce-scatter.2.cloned.1.call-start = ((), (), s32[]{:S(2)}) async-start(), calls=%async_computation.2 | async-start | bytes 4259840 | tf_op jit(solution)/shard_map/reduce_scatter | solution.py:90
  51.8 127.5 %copy-start = (bf16[1,128,8192]{2,1,0:T(8,128)(2,1)S(1)}, bf16[1,128,8192]{2,1,0:T(8,128)(2,1)}, u32[]{:S(2)}) copy-start(bf16[1,128,8192]{2,1,0:T(8,128)(2,1)} %param.11) | copy-start | bytes 6291460
  183.3 36.7 %collective-permute-start = (bf16[128,8192]{1,0:T(8,128)(2,1)}, bf16[128,8192]{1,0:T(8,128)(2,1)}, u32[]{:S(2)}, u32[]{:S(2)}) collective-permute-start(bf16[128,8192]{1,0:T(8,128)(2,1)} %get-tuple-element.300), channel_id=1, source_target_pairs={{64,0},{128,64},{192,128},{256,192},{320,256},{384,320},{448,384},... | collective-permute-start | bytes 6291464 | tf_op jit(solution)/shard_map/while/body/eval_jaxpr/ppermute | solution.py:19
  223.9 27.7 %collective-permute-start = (bf16[128,8192]{1,0:T(8,128)(2,1)}, bf16[128,8192]{1,0:T(8,128)(2,1)}, u32[]{:S(2)}, u32[]{:S(2)}) collective-permute-start(bf16[128,8192]{1,0:T(8,128)(2,1)} %get-tuple-element.300), channel_id=1, source_target_pairs={{64,0},{128,64},{192,128},{256,192},{320,256},{384,320},{448,384},... | collective-permute-start | bytes 6291464 | tf_op jit(solution)/shard_map/while/body/eval_jaxpr/ppermute | solution.py:19
  255.4 27.7 %collective-permute-start = (bf16[128,8192]{1,0:T(8,128)(2,1)}, bf16[128,8192]{1,0:T(8,128)(2,1)}, u32[]{:S(2)}, u32[]{:S(2)}) collective-permute-start(bf16[128,8192]{1,0:T(8,128)(2,1)} %get-tuple-element.300), channel_id=1, source_target_pairs={{64,0},{128,64},{192,128},{256,192},{320,256},{384,320},{448,384},... | collective-permute-start | bytes 6291464 | tf_op jit(solution)/shard_map/while/body/eval_jaxpr/ppermute | solution.py:19
  287.0 27.7 %collective-permute-start = (bf16[128,8192]{1,0:T(8,128)(2,1)}, bf16[128,8192]{1,0:T(8,128)(2,1)}, u32[]{:S(2)}, u32[]{:S(2)}) collective-permute-start(bf16[128,8192]{1,0:T(8,128)(2,1)} %get-tuple-element.300), channel_id=1, source_target_pairs={{64,0},{128,64},{192,128},{256,192},{320,256},{384,320},{448,384},... | collective-permute-start | bytes 6291464 | tf_op jit(solution)/shard_map/while/body/eval_jaxpr/ppermute | solution.py:19
  318.6 27.7 %collective-permute-start = (bf16[128,8192]{1,0:T(8,128)(2,1)}, bf16[128,8192]{1,0:T(8,128)(2,1)}, u32[]{:S(2)}, u32[]{:S(2)}) collective-permute-start(bf16[128,8192]{1,0:T(8,128)(2,1)} %get-tuple-element.300), channel_id=1, source_target_pairs={{64,0},{128,64},{192,128},{256,192},{320,256},{384,320},{448,384},... | collective-permute-start | bytes 6291464 | tf_op jit(solution)/shard_map/while/body/eval_jaxpr/ppermute | solution.py:19
  350.1 32.4 %collective-permute-start = (bf16[128,8192]{1,0:T(8,128)(2,1)}, bf16[128,8192]{1,0:T(8,128)(2,1)}, u32[]{:S(2)}, u32[]{:S(2)}) collective-permute-start(bf16[128,8192]{1,0:T(8,128)(2,1)} %get-tuple-element.300), channel_id=1, source_target_pairs={{64,0},{128,64},{192,128},{256,192},{320,256},{384,320},{448,384},... | collective-permute-start | bytes 6291464 | tf_op jit(solution)/shard_map/while/body/eval_jaxpr/ppermute | solution.py:19
  382.5 2.2 copy-start.2
  384.7 2.2 copy-start.1
  393.0 27.7 %collective-permute-start = (bf16[128,8192]{1,0:T(8,128)(2,1)}, bf16[128,8192]{1,0:T(8,128)(2,1)}, u32[]{:S(2)}, u32[]{:S(2)}) collective-permute-start(bf16[128,8192]{1,0:T(8,128)(2,1)} %get-tuple-element.300), channel_id=1, source_target_pairs={{64,0},{128,64},{192,128},{256,192},{320,256},{384,320},{448,384},... | collective-permute-start | bytes 6291464 | tf_op jit(solution)/shard_map/while/body/eval_jaxpr/ppermute | solution.py:19
  424.6 27.7 %collective-permute-start = (bf16[128,8192]{1,0:T(8,128)(2,1)}, bf16[128,8192]{1,0:T(8,128)(2,1)}, u32[]{:S(2)}, u32[]{:S(2)}) collective-permute-start(bf16[128,8192]{1,0:T(8,128)(2,1)} %get-tuple-element.300), channel_id=1, source_target_pairs={{64,0},{128,64},{192,128},{256,192},{320,256},{384,320},{448,384},... | collective-permute-start | bytes 6291464 | tf_op jit(solution)/shard_map/while/body/eval_jaxpr/ppermute | solution.py:19
  452.3 799.2 %copy-start.3 = (f32[1,2,64,128]{3,2,1,0:T(8,128)S(1)}, f32[1,2,64,128]{3,2,1,0:T(8,128)}, u32[]{:S(2)}) copy-start(f32[1,2,64,128]{3,2,1,0:T(8,128)} %param.16) | copy-start | bytes 196612
  452.3 799.2 %copy-start.4 = (f32[1,2,64,128]{3,2,1,0:T(8,128)S(1)}, f32[1,2,64,128]{3,2,1,0:T(8,128)}, u32[]{:S(2)}) copy-start(f32[1,2,64,128]{3,2,1,0:T(8,128)} %param.15) | copy-start | bytes 196612
  452.3 799.2 %copy-start.5 = (f32[1,2,64,128]{3,2,1,0:T(8,128)S(1)}, f32[1,2,64,128]{3,2,1,0:T(8,128)}, u32[]{:S(2)}) copy-start(f32[1,2,64,128]{3,2,1,0:T(8,128)} %param.14) | copy-start | bytes 196612
Sparse Core Ops, SparseCore 0:
  10.1 38.5 all-gather.3
  51.6 126.1 all-gather.5
  452.4 684.2 reduce-scatter.1
where the time goes:
time: 1260 us
  waiting for transfers between devices  1010 us (80%)
  blocking collectives  113 us (9%)
  other arithmetic  56.6 us (4%)
  local copies, waits for them, and re-layouts  29.1 us (2%)
  starting transfers between devices  25.1 us (2%)
  between operations  15.1 us (1%)
    reduce_scatter x1, waiting for transfers between devices, body(): lax.psum_scatter(gradients, 'dp', scatter_dimension=2, tiled=True)  684 us
    ppermute x8, waiting for transfers between devices, shifted(): return lax.ppermute(x, axis, pairs)  164 us
    all_gather x1, waiting for transfers between devices, body(): weights = lax.all_gather(weights_bf16[0], 'dp', axis=2, tiled=True)  126 us
    psum x1, blocking collectives, body(): square_sum = lax.psum(jnp.sum(grad_shard * grad_shard), ('pipe', 'dp'))  113 us
    add x8, other arithmetic, chain_turn(): return (gradients + grad_part, received)  46.2 us
    all_gather x1, waiting for transfers between devices, body(): loss_grad = lax.all_gather(cotangent, 'pipe', axis=1, tiled=True)  39.3 us
    another operation x15, local copies, waits for them, and re-layouts  28.9 us
  transfers between devices with their start and end apart: 11, of which 11 were waited for; matrix products, arithmetic and copies ran while one was open for 4% of the time, Pallas kernels for 0%

commit v1 on v0

--- a/solution.py
+++ b/solution.py
@@ -51,7 +51,9 @@
 def body(saved_inputs, cotangent, weights_bf16, master, moment1, moment2, valid_rows):
     sections = lax.axis_size("pipe")
     section_index = lax.axis_index("pipe")
-    weights = lax.all_gather(weights_bf16[0], "dp", axis=2, tiled=True)
+    value = weights_bf16[0]
+    outgoing_2 = jnp.stack([value] * lax.axis_size("dp"))
+    weights = jnp.concatenate(lax.all_to_all(outgoing_2, "dp", 0, 0), axis=2)
     loss_grad = lax.all_gather(cotangent, "pipe", axis=1, tiled=True)
     inputs = saved_inputs[0]
     row_count = inputs.shape[0]

time: 1260 us -> 1200 us (0.952)
  waiting for transfers between devices: 1010 us -> 938 us
  starting transfers between devices: 25.1 us -> 38 us
    all_gather x1 -> x0, waiting for transfers between devices: 126 us -> none  [body(): weights = lax.all_gather(weights_bf16[0], 'dp', axis=2, tiled=True)]
    all_to_all x0 -> x1, waiting for transfers between devices: none -> 54.3 us  [body(): weights = jnp.concatenate(lax.all_to_all(outgoing_2, 'dp', 0, 0), axis=2)]
    all_to_all x0 -> x1, starting transfers between devices: none -> 19.3 us  [body(): weights = jnp.concatenate(lax.all_to_all(outgoing_2, 'dp', 0, 0), axis=2)]
    another operation x15 -> x16, local copies, waits for them, and re-layouts: 28.9 us -> 31.6 us
where the time goes in v1:
time: 1200 us
  waiting for transfers between devices  938 us (78%)
  blocking collectives  113 us (9%)
  other arithmetic  56.6 us (5%)
  starting transfers between devices  38 us (3%)
  local copies, waits for them, and re-layouts  34.3 us (3%)
  between operations  15.4 us (1%)
    reduce_scatter x1, waiting for transfers between devices, body(): lax.psum_scatter(gradients, 'dp', scatter_dimension=2, tiled=True)  683 us
    ppermute x8, waiting for transfers between devices, shifted(): return lax.ppermute(x, axis, pairs)  164 us
    psum x1, blocking collectives, body(): square_sum = lax.psum(jnp.sum(grad_shard * grad_shard), ('pipe', 'dp'))  113 us
    all_to_all x1, waiting for transfers between devices, body(): weights = jnp.concatenate(lax.all_to_all(outgoing_2, 'dp', 0, 0), axis=2)  54.3 us
    add x8, other arithmetic, chain_turn(): return (gradients + grad_part, received)  46.2 us
    all_gather x1, waiting for transfers between devices, body(): loss_grad = lax.all_gather(cotangent, 'pipe', axis=1, tiled=True)  35.9 us
    another operation x15, local copies, waits for them, and re-layouts  28.9 us
  transfers between devices with their start and end apart: 11, of which 11 were waited for; matrix products, arithmetic and copies ran while one was open for 4% of the time, Pallas kernels for 0%

profile of v1, /device:TPU:1, one launch (start us, length us, event | category | flops | bytes accessed | tf_op | source)
XLA Modules:
  0.0 1200.7 jit_solution(9662742206500496153)
XLA Ops:
  7.2 2.6 stack.12
  9.8 19.3 %all-to-all-start = ((bf16[64,2,64,128]{3,2,1,0:T(8,128)(2,1)}), bf16[64,2,64,128]{3,2,1,0:T(8,128)(2,1)S(1)}, u32[]{:S(2)}, u32[]{:S(2)}) async-start(bf16[64,2,64,128]{3,2,1,0:T(8,128)(2,1)} %stack.12), calls=%async_computation | async-start | bytes 4194304 | tf_op jit(solution)/shard_map/all_to_all | solution.py:56
  30.5 35.9 %all-gather.2.cloned.1.call-done = bf16[128,8192]{1,0:T(8,128)(2,1)} async-done(((bf16[128,1024]{1,0:T(8,128)(2,1)}), bf16[128,8192]{1,0:T(8,128)(2,1)}) %all-gather.2.cloned.1.call-update) | async-done | bytes 2097168 | tf_op jit(solution)/shard_map/all_gather | solution.py:57
  66.5 3.2 broadcast_select_fusion.1
  69.6 54.3 %all-to-all-done = bf16[64,2,64,128]{3,2,1,0:T(8,128)(2,1)S(1)} async-done(((bf16[64,2,64,128]{3,2,1,0:T(8,128)(2,1)}), bf16[64,2,64,128]{3,2,1,0:T(8,128)(2,1)S(1)}, u32[]{:S(2)}, u32[]{:S(2)}) %all-to-all-start) | async-done | bytes 2097184 | tf_op jit(solution)/shard_map/all_to_all | solution.py:56
  127.9 266.7 %while.18 = (s32[]{:T(128)}, f32[2,64,8192]{2,1,0:T(8,128)}, bf16[128,8192]{1,0:T(8,128)(2,1)}, s32[]{:T(128)}, pred[]{:T(512)}, /*index=5*/bf16[128,8192]{1,0:T...) while((s32[]{:T(128)}, f32[2,64,8192]{2,1,0:T(8,128)}, ...), condition=%wide.region_3.4_spmd.clone, body=%wide.region_0.3_spmd.clone.sunk | while | flops 680656896 | bytes 72499496 | solution.py:91
  127.9 3.9 conditional.3
  127.9 2.4 broadcast.36
  131.8 5.3 collective-permute-start
  137.1 4.7 select_add_fusion.2
  141.8 20.5 %collective-permute-done = bf16[128,8192]{1,0:T(8,128)(2,1)} collective-permute-done((bf16[128,8192]{1,0:T(8,128)(2,1)}, bf16[128,8192]{1,0:T(8,128)(2,1)}, u32[]{:S(2)}, u32[]{:S(2)}) %collective-permute-start) | collective-permute-done | bytes 2097184 | tf_op jit(solution)/shard_map/while/body/eval_jaxpr/ppermute | solution.py:19
  162.2 3.9 conditional.3
  162.2 2.4 broadcast.36
  166.1 1.9 collective-permute-start
  168.1 5.9 select_add_fusion.2
  174.0 19.8 %collective-permute-done = bf16[128,8192]{1,0:T(8,128)(2,1)} collective-permute-done((bf16[128,8192]{1,0:T(8,128)(2,1)}, bf16[128,8192]{1,0:T(8,128)(2,1)}, u32[]{:S(2)}, u32[]{:S(2)}) %collective-permute-start) | collective-permute-done | bytes 2097184 | tf_op jit(solution)/shard_map/while/body/eval_jaxpr/ppermute | solution.py:19
  193.8 3.9 conditional.3
  193.8 2.4 broadcast.36
  197.7 1.9 collective-permute-start
  199.6 5.9 select_add_fusion.2
  205.6 19.8 %collective-permute-done = bf16[128,8192]{1,0:T(8,128)(2,1)} collective-permute-done((bf16[128,8192]{1,0:T(8,128)(2,1)}, bf16[128,8192]{1,0:T(8,128)(2,1)}, u32[]{:S(2)}, u32[]{:S(2)}) %collective-permute-start) | collective-permute-done | bytes 2097184 | tf_op jit(solution)/shard_map/while/body/eval_jaxpr/ppermute | solution.py:19
  225.4 3.9 conditional.3
  225.4 2.4 broadcast.36
  229.3 1.9 collective-permute-start
  231.2 5.9 select_add_fusion.2
  237.1 19.8 %collective-permute-done = bf16[128,8192]{1,0:T(8,128)(2,1)} collective-permute-done((bf16[128,8192]{1,0:T(8,128)(2,1)}, bf16[128,8192]{1,0:T(8,128)(2,1)}, u32[]{:S(2)}, u32[]{:S(2)}) %collective-permute-start) | collective-permute-done | bytes 2097184 | tf_op jit(solution)/shard_map/while/body/eval_jaxpr/ppermute | solution.py:19
  256.9 3.9 conditional.3
  256.9 2.4 broadcast.36
  262.8 5.9 select_add_fusion.2
  268.7 19.8 %collective-permute-done = bf16[128,8192]{1,0:T(8,128)(2,1)} collective-permute-done((bf16[128,8192]{1,0:T(8,128)(2,1)}, bf16[128,8192]{1,0:T(8,128)(2,1)}, u32[]{:S(2)}, u32[]{:S(2)}) %collective-permute-start) | collective-permute-done | bytes 2097184 | tf_op jit(solution)/shard_map/while/body/eval_jaxpr/ppermute | solution.py:19
  288.5 3.9 conditional.3
  288.5 2.4 broadcast.36
  294.4 5.9 select_add_fusion.2
  300.3 24.5 %collective-permute-done = bf16[128,8192]{1,0:T(8,128)(2,1)} collective-permute-done((bf16[128,8192]{1,0:T(8,128)(2,1)}, bf16[128,8192]{1,0:T(8,128)(2,1)}, u32[]{:S(2)}, u32[]{:S(2)}) %collective-permute-start) | collective-permute-done | bytes 2097184 | tf_op jit(solution)/shard_map/while/body/eval_jaxpr/ppermute | solution.py:19
  324.8 10.5 conditional.3
  324.8 2.2 convolution_multiply_fusion.3
  327.1 2.0 broadcast_select_fusion
  331.1 2.3 pad_maximum_fusion
  333.3 2.0 fusion.1
  335.4 1.9 collective-permute-start
  337.3 5.9 select_add_fusion.2
  343.2 19.8 %collective-permute-done = bf16[128,8192]{1,0:T(8,128)(2,1)} collective-permute-done((bf16[128,8192]{1,0:T(8,128)(2,1)}, bf16[128,8192]{1,0:T(8,128)(2,1)}, u32[]{:S(2)}, u32[]{:S(2)}) %collective-permute-start) | collective-permute-done | bytes 2097184 | tf_op jit(solution)/shard_map/while/body/eval_jaxpr/ppermute | solution.py:19
  363.0 3.9 conditional.3
  363.0 2.4 broadcast.36
  368.9 5.9 select_add_fusion.2
  374.8 19.8 %collective-permute-done = bf16[128,8192]{1,0:T(8,128)(2,1)} collective-permute-done((bf16[128,8192]{1,0:T(8,128)(2,1)}, bf16[128,8192]{1,0:T(8,128)(2,1)}, u32[]{:S(2)}, u32[]{:S(2)}) %collective-permute-start) | collective-permute-done | bytes 2097184 | tf_op jit(solution)/shard_map/while/body/eval_jaxpr/ppermute | solution.py:19
  394.6 682.9 %reduce-scatter.2.cloned.1.call-done = f32[2,64,128]{2,1,0:T(8,128)} async-done(((f32[2,64,8192]{2,1,0:T(8,128)}), f32[2,64,128]{2,1,0:T(8,128)}) %reduce-scatter.2.cloned.1.call-update) | async-done | bytes 65552 | tf_op jit(solution)/shard_map/reduce_scatter | solution.py:92
  1079.0 112.6 %psum.7 = f32[]{:T(128)} all-reduce(f32[]{:T(128)} %multiply_reduce_fusion), channel_id=1, replica_groups=mesh['pipe'=8,'dp'=64] {'pipe','dp'}, use_global_device_ids=true, to_apply=%region_6.7 | all-reduce | flops 1 | bytes 8 | tf_op jit(solution)/shard_map/psum | solution.py:93
  (35 shorter events, 26.1 us)
Async XLA Ops:
  9.8 114.1 %all-to-all-start = ((bf16[64,2,64,128]{3,2,1,0:T(8,128)(2,1)}), bf16[64,2,64,128]{3,2,1,0:T(8,128)(2,1)S(1)}, u32[]{:S(2)}, u32[]{:S(2)}) async-start(bf16[64,2,64,128]{3,2,1,0:T(8,128)(2,1)} %stack.12), calls=%async_computation | async-start | bytes 4194304 | tf_op jit(solution)/shard_map/all_to_all | solution.py:56
  29.1 37.4 %all-gather.2.cloned.1.call-start = ((), (), s32[]{:S(2)}) async-start(), calls=%async_computation.2 | async-start | bytes 2359296 | tf_op jit(solution)/shard_map/all_gather | solution.py:57
  29.8 1047.8 %reduce-scatter.2.cloned.1.call-start = ((), (), s32[]{:S(2)}) async-start(), calls=%async_computation.3 | async-start | bytes 4259840 | tf_op jit(solution)/shard_map/reduce_scatter | solution.py:92
  125.5 2.3 copy-start
  131.8 30.4 %collective-permute-start = (bf16[128,8192]{1,0:T(8,128)(2,1)}, bf16[128,8192]{1,0:T(8,128)(2,1)}, u32[]{:S(2)}, u32[]{:S(2)}) collective-permute-start(bf16[128,8192]{1,0:T(8,128)(2,1)} %get-tuple-element.300), channel_id=1, source_target_pairs={{64,0},{128,64},{192,128},{256,192},{320,256},{384,320},{448,384},... | collective-permute-start | bytes 6291464 | tf_op jit(solution)/shard_map/while/body/eval_jaxpr/ppermute | solution.py:19
  166.1 27.7 %collective-permute-start = (bf16[128,8192]{1,0:T(8,128)(2,1)}, bf16[128,8192]{1,0:T(8,128)(2,1)}, u32[]{:S(2)}, u32[]{:S(2)}) collective-permute-start(bf16[128,8192]{1,0:T(8,128)(2,1)} %get-tuple-element.300), channel_id=1, source_target_pairs={{64,0},{128,64},{192,128},{256,192},{320,256},{384,320},{448,384},... | collective-permute-start | bytes 6291464 | tf_op jit(solution)/shard_map/while/body/eval_jaxpr/ppermute | solution.py:19
  197.7 27.7 %collective-permute-start = (bf16[128,8192]{1,0:T(8,128)(2,1)}, bf16[128,8192]{1,0:T(8,128)(2,1)}, u32[]{:S(2)}, u32[]{:S(2)}) collective-permute-start(bf16[128,8192]{1,0:T(8,128)(2,1)} %get-tuple-element.300), channel_id=1, source_target_pairs={{64,0},{128,64},{192,128},{256,192},{320,256},{384,320},{448,384},... | collective-permute-start | bytes 6291464 | tf_op jit(solution)/shard_map/while/body/eval_jaxpr/ppermute | solution.py:19
  229.3 27.7 %collective-permute-start = (bf16[128,8192]{1,0:T(8,128)(2,1)}, bf16[128,8192]{1,0:T(8,128)(2,1)}, u32[]{:S(2)}, u32[]{:S(2)}) collective-permute-start(bf16[128,8192]{1,0:T(8,128)(2,1)} %get-tuple-element.300), channel_id=1, source_target_pairs={{64,0},{128,64},{192,128},{256,192},{320,256},{384,320},{448,384},... | collective-permute-start | bytes 6291464 | tf_op jit(solution)/shard_map/while/body/eval_jaxpr/ppermute | solution.py:19
  260.9 27.7 %collective-permute-start = (bf16[128,8192]{1,0:T(8,128)(2,1)}, bf16[128,8192]{1,0:T(8,128)(2,1)}, u32[]{:S(2)}, u32[]{:S(2)}) collective-permute-start(bf16[128,8192]{1,0:T(8,128)(2,1)} %get-tuple-element.300), channel_id=1, source_target_pairs={{64,0},{128,64},{192,128},{256,192},{320,256},{384,320},{448,384},... | collective-permute-start | bytes 6291464 | tf_op jit(solution)/shard_map/while/body/eval_jaxpr/ppermute | solution.py:19
  292.4 32.4 %collective-permute-start = (bf16[128,8192]{1,0:T(8,128)(2,1)}, bf16[128,8192]{1,0:T(8,128)(2,1)}, u32[]{:S(2)}, u32[]{:S(2)}) collective-permute-start(bf16[128,8192]{1,0:T(8,128)(2,1)} %get-tuple-element.300), channel_id=1, source_target_pairs={{64,0},{128,64},{192,128},{256,192},{320,256},{384,320},{448,384},... | collective-permute-start | bytes 6291464 | tf_op jit(solution)/shard_map/while/body/eval_jaxpr/ppermute | solution.py:19
  324.8 2.2 copy-start.2
  327.1 2.2 copy-start.1
  335.4 27.7 %collective-permute-start = (bf16[128,8192]{1,0:T(8,128)(2,1)}, bf16[128,8192]{1,0:T(8,128)(2,1)}, u32[]{:S(2)}, u32[]{:S(2)}) collective-permute-start(bf16[128,8192]{1,0:T(8,128)(2,1)} %get-tuple-element.300), channel_id=1, source_target_pairs={{64,0},{128,64},{192,128},{256,192},{320,256},{384,320},{448,384},... | collective-permute-start | bytes 6291464 | tf_op jit(solution)/shard_map/while/body/eval_jaxpr/ppermute | solution.py:19
  366.9 27.7 %collective-permute-start = (bf16[128,8192]{1,0:T(8,128)(2,1)}, bf16[128,8192]{1,0:T(8,128)(2,1)}, u32[]{:S(2)}, u32[]{:S(2)}) collective-permute-start(bf16[128,8192]{1,0:T(8,128)(2,1)} %get-tuple-element.300), channel_id=1, source_target_pairs={{64,0},{128,64},{192,128},{256,192},{320,256},{384,320},{448,384},... | collective-permute-start | bytes 6291464 | tf_op jit(solution)/shard_map/while/body/eval_jaxpr/ppermute | solution.py:19
  394.6 797.7 %copy-start.3 = (f32[1,2,64,128]{3,2,1,0:T(8,128)S(1)}, f32[1,2,64,128]{3,2,1,0:T(8,128)}, u32[]{:S(2)}) copy-start(f32[1,2,64,128]{3,2,1,0:T(8,128)} %param.16) | copy-start | bytes 196612
  394.6 797.7 %copy-start.4 = (f32[1,2,64,128]{3,2,1,0:T(8,128)S(1)}, f32[1,2,64,128]{3,2,1,0:T(8,128)}, u32[]{:S(2)}) copy-start(f32[1,2,64,128]{3,2,1,0:T(8,128)} %param.15) | copy-start | bytes 196612
  394.6 797.7 %copy-start.5 = (f32[1,2,64,128]{3,2,1,0:T(8,128)S(1)}, f32[1,2,64,128]{3,2,1,0:T(8,128)}, u32[]{:S(2)}) copy-start(f32[1,2,64,128]{3,2,1,0:T(8,128)} %param.14) | copy-start | bytes 196612
Sparse Core Ops, SparseCore 0:
  32.0 34.3 all-gather.1
  394.7 682.7 reduce-scatter.1
